TPU v7x, 32 devices: a whole 2x2x4 slice. The times are simulated.
32 devices in a mesh: space: 8 (over y, x, core), mp: 4 (over z).
Axes of the slice: x: 2, y: 2, z: 4, core: 2. Of those that a mesh axis runs over, the one named last changes fastest.
Arguments:
- tokens: bfloat16 [12288, 1024], P('space')
- norm_gain: float32 [1024], replicated, may hold values from 0.5 to 1.5
- w_qkv: bfloat16 [1024, 4, 192], P(None, 'mp')
- w_out: bfloat16 [256, 1024], replicated, may hold values from -0.75 to 0.75
- head_scale: float32 [4], P('mp'), may hold values from 8 to 400
- cycle_to_nested: int32 [12288], P('space'), may hold values from 0 to 12287, as said below
- neighbours: int32 [96, 9], P('space'), may hold values from -1 to 95, as said below
Outputs:
- mixed: bfloat16 [12288, 1024], P(('space', 'mp'))
Inputs may be any that keep to these rules, and one draw needn't show every extreme that they name: `cycle_to_nested`: A permutation of the tokens; the cycle rows of each index of space hold exactly 192 of the nested places of each index of space, the block of 1536 places of that index. `neighbours`: slot 0 names the block itself; the other slots name distinct other blocks at most 6 places away in block order, counted around the end of the order; only slots 7 and 8 may be -1.
All inputs are finite; a program needn't handle non-finite values.
Results may differ from a plain program's by a relative error of at most 0.012.
The roundings to bfloat16 on the way count: a program that leaves them out, or rounds other values in their place, can miss the bound.
Values may be sent and summed in bfloat16 or wider, within the bound.
No kernel may reach another device: no remote copies, remote signals or barrier semaphores. Data moves between devices by JAX's collectives and lax.ppermute only.
A program may use at most 64 MiB of HBM per device.

v0:
```python
import jax
import jax.numpy as jnp
from jax import lax
from jax.sharding import PartitionSpec as P

BLOCK = 128
REACH = 6


def extended_2(shard, sides, width):
    for axis, dim in sides:
        size, length = (lax.axis_size(axis), shard.shape[dim])
        up = [(i, (i + 1) % size) for i in range(size)]
        down = [(j, i) for i, j in up]
        last = lax.slice_in_dim(shard, length - width, length, axis=dim)
        leading = lax.slice_in_dim(shard, 0, width, axis=dim)
        before = lax.ppermute(last, axis, up)
        after = lax.ppermute(leading, axis, down)
        shard = jnp.concatenate([before, shard, after], axis=dim)
    return shard


def norm_rows(tokens, norm_gain):
    values = tokens.astype(jnp.float32)
    mean_square = jnp.mean(values * values, axis=1, keepdims=True)
    return (values * lax.rsqrt(mean_square + 1e-05) * norm_gain).astype(jnp.bfloat16)


def project_head(normed, weight_head, scale_value, head_dim):
    projected = jnp.dot(normed, weight_head, preferred_element_type=jnp.float32)
    query_rows = projected[:, :head_dim]
    key_raw = projected[:, head_dim : 2 * head_dim]
    values = projected[:, 2 * head_dim :]
    query_rows = query_rows * (
        scale_value * lax.rsqrt(jnp.sum(query_rows * query_rows, axis=1, keepdims=True) + 1e-06)
    )
    key_raw = key_raw * lax.rsqrt(jnp.sum(key_raw * key_raw, axis=1, keepdims=True) + 1e-06)
    return jnp.concatenate([query_rows, key_raw, values], axis=1).astype(jnp.bfloat16)


def attend_blocks(query_rows, kv_blocks, positions, present, head_dim):
    block_rows = query_rows.shape[1]
    gathered = kv_blocks[positions]
    batch_blocks = gathered.shape[0]
    gathered_key_rows = gathered[..., :head_dim].reshape(batch_blocks, -1, head_dim)
    gathered_value_rows = gathered[..., head_dim:].reshape(batch_blocks, -1, head_dim)
    score_matrix = jnp.einsum(
        "ltv,lpv->ltp", query_rows, gathered_key_rows, preferred_element_type=jnp.float32
    )
    key_mask = jnp.repeat(present, block_rows, axis=1)[:, None, :]
    score_matrix = jnp.where(key_mask, score_matrix, -1e30)
    row_max = jnp.max(score_matrix, axis=2, keepdims=True)
    exponent = jnp.exp(score_matrix - row_max)
    row_total = jnp.sum(exponent, axis=2, keepdims=True)
    attention_weight = exponent.astype(jnp.bfloat16)
    weighted_sum = jnp.einsum(
        "uct,uth->uch", attention_weight, gathered_value_rows, preferred_element_type=jnp.float32
    )
    return (weighted_sum / row_total).astype(jnp.bfloat16)


def per_device(tokens, norm_gain, w_qkv, w_out, head_scale, cycle_to_nested, neighbours):
    tok_dev, model_width = tokens.shape
    space_count = lax.axis_size("space")
    head_dim = w_qkv.shape[2] // 3
    weight_head = w_qkv.reshape(model_width, 3 * head_dim)
    normed = norm_rows(tokens, norm_gain)
    row_order = jnp.argsort(cycle_to_nested)
    group_rows = tok_dev // space_count
    send_slots = cycle_to_nested[row_order].reshape(space_count, group_rows)
    base_slot = lax.axis_index("space") * tok_dev
    packed = project_head(normed, weight_head, head_scale[0], head_dim)
    send_rows = packed[row_order].reshape(space_count, group_rows, 3 * head_dim)
    got_rows, got_slots = (
        lax.all_to_all(send_rows, "space", split_axis=0, concat_axis=0, tiled=True),
        lax.all_to_all(send_slots, "space", split_axis=0, concat_axis=0, tiled=True),
    )
    slot_local = got_slots.reshape(-1) - base_slot
    nested_ordering = (
        jnp.zeros_like(packed).at[slot_local].set(got_rows.reshape(tok_dev, 3 * head_dim))
    )
    query_rows = nested_ordering[:, :head_dim].reshape(-1, BLOCK, head_dim)
    key_vals = nested_ordering[:, head_dim:]
    blk_count = tok_dev // BLOCK
    padding_blocks = REACH
    extended = extended_2(key_vals, (("space", 0),), REACH * BLOCK)
    kv_blocks = extended.reshape(blk_count + 2 * padding_blocks, BLOCK, 2 * head_dim)
    cycle_blocks = blk_count * space_count
    half_cycle = cycle_blocks // 2
    relative = (
        jnp.mod(neighbours - lax.axis_index("space") * blk_count + half_cycle, cycle_blocks)
        - half_cycle
    )
    present = neighbours >= 0
    positions = jnp.where(present, relative + padding_blocks, 0)
    attn = attend_blocks(query_rows, kv_blocks, positions, present, head_dim).reshape(
        tok_dev, head_dim
    )
    head_rows = lax.all_to_all(attn, "mp", split_axis=0, concat_axis=1, tiled=True)
    return jnp.dot(head_rows, w_out, preferred_element_type=jnp.float32).astype(jnp.bfloat16)


def solution(mesh):
    placed = (
        P("space", None),
        P(),
        P(None, "mp", None),
        P(),
        P("mp"),
        P("space"),
        P("space", None),
    )
    return jax.shard_map(
        per_device, mesh=mesh, in_specs=placed, out_specs=P(("space", "mp"), None), check_vma=False
    )
```

profile of v0, /device:TPU:0, one launch (start us, length us, event | category | flops | bytes accessed | tf_op | source)
XLA Modules:
  0.0 90.3 jit_solution(2709928269623220711)
XLA Ops:
  0.0 5.8 %sort.17 = (s32[1536]{0:T(1024)}, s32[1536]{0:T(1024)S(1)}) sort(s32[1536]{0:T(1024)} %param.12, s32[1536]{0:T(1024)S(1)} %iota.4), dimensions={0}, to_apply=%region_0.0 | sort | flops 16896 | bytes 24576 | tf_op jit(solution)/shard_map/jit(argsort)/sort | solution.py:68
  5.9 8.4 %gather_fusion = s32[1536]{0:T(1024)S(1)} fusion(s32[1536]{0:T(1024)S(1)} %copy-done.1, s32[2048]{0:T(1024)S(1)} %pad_clamp_fusion), kind=kCustom, calls=%fused_computation | custom fusion | bytes 18432 | tf_op jit(solution)/shard_map/gather | solution.py:70
  14.2 0.7 all_to_all.23
  14.9 5.2 %all-to-all-start = ((s32[8,1,192]{2,1,0:T(1,128)}), s32[8,1,192]{2,1,0:T(1,128)S(1)}, u32[]{:S(2)}, u32[]{:S(2)}) async-start(s32[8,1,192]{2,1,0:T(1,128)} %all_to_all.23), calls=%async_computation | async-start | bytes 16384 | tf_op jit(solution)/shard_map/all_to_all | solution.py:76
  20.1 2.6 %fusion = f32[1536]{0:T(1024)S(1)} fusion(bf16[1536,1024]{1,0:T(8,128)(2,1)} %param.7), kind=kLoop, calls=%fused_computation.8 | loop fusion | flops 4717056 | bytes 3151872 | tf_op jit(solution)/shard_map/reduce_sum | solution.py:25
  22.7 3.2 %fusion.10 = f32[1536,192]{0,1:T(8,128)S(1)} fusion(bf16[1536,1024]{1,0:T(8,128)(2,1)} %param.7, f32[1024]{0:T(1024)S(1)} %copy-done.5, f32[1536]{0:T(1024)S(1)} %add_rsqrt_fusion.1, bf16[1024,1,192]{0,2,1:T(8,128)(2,1)S(1)} %copy-done.4), kind=kOutput, calls=%fused_computation.17 | convolution fusion | flops 610271232 | bytes 4728832 | tf_op jit(solution)/shard_map/dot_general | solution.py:30
  26.8 0.3 copy.23
  27.1 5.4 %gather_fusion.1 = bf16[1536,192]{1,0:T(8,128)(2,1)} fusion(bf16[1536,192]{1,0:T(8,128)(2,1)S(1)} %copy.23, s32[2048]{0:T(1024)S(1)} %pad_clamp_fusion), kind=kCustom, calls=%fused_computation.1 | custom fusion | bytes 1185792 | tf_op jit(solution)/shard_map/gather | solution.py:73
  32.4 4.2 %all-to-all-start.1 = ((bf16[8,192,192]{2,1,0:T(8,128)(2,1)}), bf16[8,192,192]{2,1,0:T(8,128)(2,1)S(1)}, u32[]{:S(2)}, u32[]{:S(2)}) async-start(bf16[8,192,192]{2,1,0:T(8,128)(2,1)} %bitcast.2), calls=%async_computation.1 | async-start | bytes 1572864 | tf_op jit(solution)/shard_map/all_to_all | solution.py:75
  36.8 12.4 %all-to-all-done.1 = bf16[8,192,192]{2,1,0:T(8,128)(2,1)S(1)} async-done(((bf16[8,192,192]{2,1,0:T(8,128)(2,1)}), bf16[8,192,192]{2,1,0:T(8,128)(2,1)S(1)}, u32[]{:S(2)}, u32[]{:S(2)}) %all-to-all-start.1) | async-done | bytes 589856 | tf_op jit(solution)/shard_map/all_to_all | solution.py:75
  49.2 7.3 %scatter_custom_fusion = bf16[1536,192]{1,0:T(8,128)(2,1)S(1)} fusion(s32[1536]{0:T(1024)S(1)} %fusion.25, bf16[1536,192]{1,0:T(8,128)(2,1)S(1)} %bitcast.31, bf16[]{:T(256)} %constant.17.clone.1), kind=kCustom, calls=%fused_computation.31 | custom fusion | bytes 589826 | tf_op jit(solution)/shard_map/scatter | solution.py:80
  56.5 0.2 fusion.28
  56.8 2.6 %collective-permute-start.1 = (bf16[768,128]{1,0:T(8,128)(2,1)S(1)}, bf16[768,128]{1,0:T(8,128)(2,1)S(1)}, u32[]{:S(2)}, u32[]{:S(2)}) collective-permute-start(bf16[768,128]{1,0:T(8,128)(2,1)S(1)} %get-tuple-element.14), channel_id=1, source_target_pairs={{4,0},{8,4},{12,8},{16,12},{20,16},{24,20},{28,24},{0,28},{5,1},{9... | collective-permute-start | bytes 589832 | tf_op jit(solution)/shard_map/ppermute | solution.py:18
  59.7 0.2 slice.50
  59.8 5.0 %collective-permute-done = bf16[768,128]{1,0:T(8,128)(2,1)S(1)} collective-permute-done((bf16[768,128]{1,0:T(8,128)(2,1)S(1)}, bf16[768,128]{1,0:T(8,128)(2,1)S(1)}, u32[]{:S(2)}, u32[]{:S(2)}) %collective-permute-start) | collective-permute-done | bytes 196640 | tf_op jit(solution)/shard_map/ppermute | solution.py:17
  64.9 2.8 %gather_fusion.2 = bf16[108,128,128]{2,1,0:T(8,128)(2,1)} fusion(bf16[24,128,128]{2,1,0:T(8,128)(2,1)S(1)} %bitcast.27, s32[1024]{0:T(1024)S(1)} %pad_clamp_fusion.1), kind=kCustom, calls=%fused_computation.2 | custom fusion | bytes 7078320 | tf_op jit(solution)/shard_map/gather | solution.py:43
  67.7 4.5 %fusion.27 = (bf16[12,9,128,64]{3,2,1,0:T(8,128)(2,1)S(1)}, bf16[12,9,128,64]{3,2,1,0:T(8,128)(2,1)S(1)}) fusion(bf16[12,9,128,128]{3,2,1,0:T(8,128)(2,1)} %bitcast.26), kind=kLoop, calls=%fused_computation.49 | loop fusion | bytes 7077888 | tf_op jit(solution)/shard_map/slice | solution.py:45
  72.2 1.3 %select_reduce_fusion = (f32[12,128]{1,0:T(8,128)S(1)}, f32[12,128,1152]{2,1,0:T(8,128)S(1)}) fusion(pred[12,1152]{1,0:T(8,128)(4,1)S(1)} %bitcast.33, bf16[12,128,64]{2,1,0:T(8,128)(2,1)S(1)} %bitcast.29, bf16[12,1152,64]{2,1,0:T(8,128)(2,1)S(1)} %bitcast.28), kind=kOutput, calls=%fused_computation.7 | convolution fusion | flops 230029824 | bytes 9063936 | tf_op jit(solution)/shard_map/ltv,lpv->ltp/dot_general | solution.py:47
  73.5 1.7 %fusion.3 = f32[12,128]{1,0:T(8,128)S(1)} fusion(f32[12,128,1152]{2,1,0:T(8,128)S(1)} %get-tuple-element.16, f32[12,128]{1,0:T(8,128)S(1)} %get-tuple-element.15, pred[12,1152]{1,0:T(8,128)(4,1)S(1)} %bitcast.34), kind=kLoop, calls=%fused_computation.11 | loop fusion | flops 5306880 | bytes 7104000 | tf_op jit(solution)/shard_map/reduce_sum | solution.py:54
  75.2 2.0 %fusion.17 = bf16[12,128,64]{1,2,0:T(8,128)(2,1)S(1)} fusion(bf16[12,1152,64]{2,1,0:T(8,128)(2,1)S(1)} %bitcast.30, f32[12,128,1152]{2,1,0:T(8,128)S(1)} %get-tuple-element.16, f32[12,128]{1,0:T(8,128)S(1)} %get-tuple-element.15, pred[12,1152]{1,0:T(8,128)(4,1)S(1)} %bitcast.35, f32[12,128]{1,0:T(8,128)S(1)} %fusion.3), kind=kOutput, calls=%fused_computation.22 | convolution fusion | flops 231997440 | bytes 9070080 | tf_op jit(solution)/shard_map/uct,uth->uch/dot_general | solution.py:56
  77.2 0.1 copy.28
  77.3 0.1 all_to_all.26
  77.5 11.6 %all_to_all.33 = bf16[4,384,64]{1,2,0:T(8,128)(2,1)S(1)} all-to-all(bf16[4,384,64]{1,2,0:T(8,128)(2,1)S(1)} %copy.29), channel_id=1, replica_groups=mesh['space'=8,'mp'=4] {'mp'}, dimensions={0} | all-to-all | bytes 393216 | tf_op jit(solution)/shard_map/all_to_all | solution.py:99
  89.1 1.3 %convolution_convert_fusion = bf16[384,1024]{1,0:T(8,128)(2,1)} fusion(bf16[384,256]{0,1:T(8,128)(2,1)S(1)} %bitcast.32, bf16[256,1024]{1,0:T(8,128)(2,1)S(1)} %copy-done), kind=kOutput, calls=%fused_computation.20 | convolution fusion | flops 201719808 | bytes 1507328 | tf_op jit(solution)/shard_map/dot_general | solution.py:100
  (38 shorter events, 0.8 us)
Async XLA Ops:
  0.0 89.1 %copy-start = (bf16[256,1024]{1,0:T(8,128)(2,1)S(1)}, bf16[256,1024]{1,0:T(8,128)(2,1)}, u32[]{:S(2)}) copy-start(bf16[256,1024]{1,0:T(8,128)(2,1)} %param.10) | copy-start | bytes 1572868
  0.0 5.8 %copy-start.1 = (s32[1536]{0:T(1024)S(1)}, s32[1536]{0:T(1024)}, u32[]{:S(2)}) copy-start(s32[1536]{0:T(1024)} %param.12) | copy-start | bytes 18436
  5.8 16.9 %copy-start.4 = (bf16[1024,1,192]{0,2,1:T(8,128)(2,1)S(1)}, bf16[1024,1,192]{0,2,1:T(8,128)(2,1)}, u32[]{:S(2)}) copy-start(bf16[1024,1,192]{0,2,1:T(8,128)(2,1)} %param.9) | copy-start | bytes 1179652
  5.8 16.9 %copy-start.5 = (f32[1024]{0:T(1024)S(1)}, f32[1024]{0:T(1024)}, u32[]{:S(2)}) copy-start(f32[1024]{0:T(1024)} %param.8) | copy-start | bytes 12292
  14.9 17.5 %all-to-all-start = ((s32[8,1,192]{2,1,0:T(1,128)}), s32[8,1,192]{2,1,0:T(1,128)S(1)}, u32[]{:S(2)}, u32[]{:S(2)}) async-start(s32[8,1,192]{2,1,0:T(1,128)} %all_to_all.23), calls=%async_computation | async-start | bytes 16384 | tf_op jit(solution)/shard_map/all_to_all | solution.py:76
  27.1 9.6 %copy-start.3 = (s32[12,9]{1,0:T(8,128)S(1)}, s32[12,9]{1,0:T(8,128)}, u32[]{:S(2)}) copy-start(s32[12,9]{1,0:T(8,128)} %param.13) | copy-start | bytes 1300
  32.4 16.8 %all-to-all-start.1 = ((bf16[8,192,192]{2,1,0:T(8,128)(2,1)}), bf16[8,192,192]{2,1,0:T(8,128)(2,1)S(1)}, u32[]{:S(2)}, u32[]{:S(2)}) async-start(bf16[8,192,192]{2,1,0:T(8,128)(2,1)} %bitcast.2), calls=%async_computation.1 | async-start | bytes 1572864 | tf_op jit(solution)/shard_map/all_to_all | solution.py:75
  56.5 11.2 %copy-start.2 = (bf16[1536,192]{1,0:T(8,128)(2,1)}, bf16[1536,192]{1,0:T(8,128)(2,1)S(1)}, u32[]{:S(2)}) copy-start(bf16[1536,192]{1,0:T(8,128)(2,1)S(1)} %scatter_custom_fusion) | copy-start | bytes 1769476
  56.7 8.1 %collective-permute-start = (bf16[768,128]{1,0:T(8,128)(2,1)S(1)}, bf16[768,128]{1,0:T(8,128)(2,1)S(1)}, u32[]{:S(2)}, u32[]{:S(2)}) collective-permute-start(bf16[768,128]{1,0:T(8,128)(2,1)S(1)} %get-tuple-element.13), channel_id=1, source_target_pairs={{0,4},{4,8},{8,12},{12,16},{16,20},{20,24},{24,28},{28,0},{1,5},{5... | collective-permute-start | bytes 589832 | tf_op jit(solution)/shard_map/ppermute | solution.py:17
  56.8 8.1 %collective-permute-start.1 = (bf16[768,128]{1,0:T(8,128)(2,1)S(1)}, bf16[768,128]{1,0:T(8,128)(2,1)S(1)}, u32[]{:S(2)}, u32[]{:S(2)}) collective-permute-start(bf16[768,128]{1,0:T(8,128)(2,1)S(1)} %get-tuple-element.14), channel_id=1, source_target_pairs={{4,0},{8,4},{12,8},{16,12},{20,16},{24,20},{28,24},{0,28},{5,1},{9... | collective-permute-start | bytes 589832 | tf_op jit(solution)/shard_map/ppermute | solution.py:18
  67.7 4.5 %slice-start = ((bf16[1536,192]{1,0:T(8,128)(2,1)}), bf16[1536,64]{1,0:T(8,128)(2,1)S(1)}, s32[]{:S(2)}) async-start(bf16[1536,192]{1,0:T(8,128)(2,1)} %copy-done.2), calls=%async_computation.3 | async-start | bytes 786432 | tf_op jit(solution)/shard_map/slice | solution.py:82
where the time goes:
time: 90.7 us; the launch traced here: 90.3 us
  local copies, waits for them, and re-layouts  30.3 us (33%)
  waiting for transfers between devices  17.4 us (19%)
  starting transfers between devices  12.1 us (13%)
  blocking collectives  11.6 us (13%)
  other arithmetic  10.4 us (11%)
  matrix products  7.71 us (9%)
  between operations  0.91 us (1%)
    all_to_all x1, waiting for transfers between devices, per_device(): lax.all_to_all(send_rows, 'space', split_axis=0, concat_axis=0, tiled=True)  12.4 us
    all_to_all x1, blocking collectives, per_device(): lax.all_to_all(attn, 'mp', split_axis=0, concat_axis=1, tiled=True)  11.6 us
    gather x1, local copies, waits for them, and re-layouts, per_device(): send_slots = cycle_to_nested[row_order].reshape(space_count, group_rows)  8.39 us
    scatter x1, local copies, waits for them, and re-layouts, per_device(): jnp.zeros_like(packed).at[slot_local]  7.32 us
    sort x1, other arithmetic, per_device(): row_order = jnp.argsort(cycle_to_nested)  5.8 us
    gather x1, local copies, waits for them, and re-layouts, per_device(): send_rows = packed[row_order].reshape(space_count, group_rows, 3 * head_dim)  5.36 us
    all_to_all x1, starting transfers between devices, per_device(): lax.all_to_all(send_slots, 'space', split_axis=0, concat_axis=0, tiled=True)  5.2 us
    ppermute x1, waiting for transfers between devices, extended_2(): before = lax.ppermute(last, axis, up)  4.99 us
  transfers between devices with their start and end apart: 4, of which 2 were waited for; matrix products, arithmetic and copies ran while one was open for 13% of the time, Pallas kernels for 0%

commit v1 on v0

--- a/solution.py
+++ b/solution.py
@@ -96,7 +96,9 @@
     attn = attend_blocks(query_rows, kv_blocks, positions, present, head_dim).reshape(
         tok_dev, head_dim
     )
-    head_rows = lax.all_to_all(attn, "mp", split_axis=0, concat_axis=1, tiled=True)
+    pieces = jnp.split(attn, lax.axis_size("mp"), axis=0)
+    arrived = lax.all_to_all(jnp.stack(pieces), "mp", 0, 0)
+    head_rows = jnp.concatenate(arrived, axis=1)
     return jnp.dot(head_rows, w_out, preferred_element_type=jnp.float32).astype(jnp.bfloat16)
 
 

time: 90.7 us -> 90.9 us (level)
  no operation moved by 1% of the time
where the time goes in v1:
time: 90.9 us; the launch traced here: 90.5 us
  local copies, waits for them, and re-layouts  30.4 us (33%)
  waiting for transfers between devices  17.4 us (19%)
  starting transfers between devices  12.1 us (13%)
  blocking collectives  11.6 us (13%)
  other arithmetic  10.4 us (11%)
  matrix products  7.71 us (8%)
  between operations  0.94 us (1%)
    all_to_all x1, waiting for transfers between devices, per_device(): lax.all_to_all(send_rows, 'space', split_axis=0, concat_axis=0, tiled=True)  12.4 us
    all_to_all x1, blocking collectives, per_device(): arrived = lax.all_to_all(jnp.stack(pieces), 'mp', 0, 0)  11.6 us
    gather x1, local copies, waits for them, and re-layouts, per_device(): send_slots = cycle_to_nested[row_order].reshape(space_count, group_rows)  8.39 us
    scatter x1, local copies, waits for them, and re-layouts, per_device(): jnp.zeros_like(packed).at[slot_local]  7.32 us
    sort x1, other arithmetic, per_device(): row_order = jnp.argsort(cycle_to_nested)  5.8 us
    gather x1, local copies, waits for them, and re-layouts, per_device(): send_rows = packed[row_order].reshape(space_count, group_rows, 3 * head_dim)  5.36 us
    all_to_all x1, starting transfers between devices, per_device(): lax.all_to_all(send_slots, 'space', split_axis=0, concat_axis=0, tiled=True)  5.2 us
    ppermute x1, waiting for transfers between devices, extended_2(): before = lax.ppermute(last, axis, up)  4.99 us
  transfers between devices with their start and end apart: 4, of which 2 were waited for; matrix products, arithmetic and copies ran while one was open for 13% of the time, Pallas kernels for 0%

profile of v1, /device:TPU:0, one launch (start us, length us, event | category | flops | bytes accessed | tf_op | source)
XLA Modules:
  0.0 90.5 jit_solution(6265551992363898701)
XLA Ops:
  0.0 5.8 %sort.17 = (s32[1536]{0:T(1024)}, s32[1536]{0:T(1024)S(1)}) sort(s32[1536]{0:T(1024)} %param.12, s32[1536]{0:T(1024)S(1)} %iota.4), dimensions={0}, to_apply=%region_0.0 | sort | flops 16896 | bytes 24576 | tf_op jit(solution)/shard_map/jit(argsort)/sort | solution.py:68
  5.9 8.4 %gather_fusion = s32[1536]{0:T(1024)S(1)} fusion(s32[1536]{0:T(1024)S(1)} %copy-done.1, s32[2048]{0:T(1024)S(1)} %pad_clamp_fusion), kind=kCustom, calls=%fused_computation | custom fusion | bytes 18432 | tf_op jit(solution)/shard_map/gather | solution.py:70
  14.2 0.7 all_to_all.12
  14.9 5.2 %all-to-all-start = ((s32[8,1,192]{2,1,0:T(1,128)}), s32[8,1,192]{2,1,0:T(1,128)S(1)}, u32[]{:S(2)}, u32[]{:S(2)}) async-start(s32[8,1,192]{2,1,0:T(1,128)} %all_to_all.12), calls=%async_computation | async-start | bytes 16384 | tf_op jit(solution)/shard_map/all_to_all | solution.py:76
  20.1 2.6 %fusion = f32[1536]{0:T(1024)S(1)} fusion(bf16[1536,1024]{1,0:T(8,128)(2,1)} %param.7), kind=kLoop, calls=%fused_computation.8 | loop fusion | flops 4717056 | bytes 3151872 | tf_op jit(solution)/shard_map/reduce_sum | solution.py:25
  22.7 3.2 %fusion.10 = f32[1536,192]{0,1:T(8,128)S(1)} fusion(bf16[1536,1024]{1,0:T(8,128)(2,1)} %param.7, f32[1024]{0:T(1024)S(1)} %copy-done.5, f32[1536]{0:T(1024)S(1)} %add_rsqrt_fusion.1, bf16[1024,1,192]{0,2,1:T(8,128)(2,1)S(1)} %copy-done.4), kind=kOutput, calls=%fused_computation.17 | convolution fusion | flops 610271232 | bytes 4728832 | tf_op jit(solution)/shard_map/dot_general | solution.py:30
  26.8 0.3 copy.18
  27.1 5.4 %gather_fusion.1 = bf16[1536,192]{1,0:T(8,128)(2,1)} fusion(bf16[1536,192]{1,0:T(8,128)(2,1)S(1)} %copy.18, s32[2048]{0:T(1024)S(1)} %pad_clamp_fusion), kind=kCustom, calls=%fused_computation.1 | custom fusion | bytes 1185792 | tf_op jit(solution)/shard_map/gather | solution.py:73
  32.4 4.2 %all-to-all-start.1 = ((bf16[8,192,192]{2,1,0:T(8,128)(2,1)}), bf16[8,192,192]{2,1,0:T(8,128)(2,1)S(1)}, u32[]{:S(2)}, u32[]{:S(2)}) async-start(bf16[8,192,192]{2,1,0:T(8,128)(2,1)} %bitcast.2), calls=%async_computation.1 | async-start | bytes 1572864 | tf_op jit(solution)/shard_map/all_to_all | solution.py:75
  36.8 12.4 %all-to-all-done.1 = bf16[8,192,192]{2,1,0:T(8,128)(2,1)S(1)} async-done(((bf16[8,192,192]{2,1,0:T(8,128)(2,1)}), bf16[8,192,192]{2,1,0:T(8,128)(2,1)S(1)}, u32[]{:S(2)}, u32[]{:S(2)}) %all-to-all-start.1) | async-done | bytes 589856 | tf_op jit(solution)/shard_map/all_to_all | solution.py:75
  49.2 7.3 %scatter_custom_fusion = bf16[1536,192]{1,0:T(8,128)(2,1)S(1)} fusion(s32[1536]{0:T(1024)S(1)} %fusion.25, bf16[1536,192]{1,0:T(8,128)(2,1)S(1)} %bitcast.37, bf16[]{:T(256)} %constant.17.clone.1), kind=kCustom, calls=%fused_computation.31 | custom fusion | bytes 589826 | tf_op jit(solution)/shard_map/scatter | solution.py:80
  56.5 0.2 fusion.28
  56.8 2.6 %collective-permute-start.1 = (bf16[768,128]{1,0:T(8,128)(2,1)S(1)}, bf16[768,128]{1,0:T(8,128)(2,1)S(1)}, u32[]{:S(2)}, u32[]{:S(2)}) collective-permute-start(bf16[768,128]{1,0:T(8,128)(2,1)S(1)} %get-tuple-element.14), channel_id=1, source_target_pairs={{4,0},{8,4},{12,8},{16,12},{20,16},{24,20},{28,24},{0,28},{5,1},{9... | collective-permute-start | bytes 589832 | tf_op jit(solution)/shard_map/ppermute | solution.py:18
  59.4 0.1 reshape.116
  59.5 0.1 broadcast_in_dim.36
  59.7 0.2 slice.54
  59.8 5.0 %collective-permute-done = bf16[768,128]{1,0:T(8,128)(2,1)S(1)} collective-permute-done((bf16[768,128]{1,0:T(8,128)(2,1)S(1)}, bf16[768,128]{1,0:T(8,128)(2,1)S(1)}, u32[]{:S(2)}, u32[]{:S(2)}) %collective-permute-start) | collective-permute-done | bytes 196640 | tf_op jit(solution)/shard_map/ppermute | solution.py:17
  64.9 2.8 %gather_fusion.2 = bf16[108,128,128]{2,1,0:T(8,128)(2,1)} fusion(bf16[24,128,128]{2,1,0:T(8,128)(2,1)S(1)} %bitcast.33, s32[1024]{0:T(1024)S(1)} %pad_clamp_fusion.1), kind=kCustom, calls=%fused_computation.2 | custom fusion | bytes 7078320 | tf_op jit(solution)/shard_map/gather | solution.py:43
  67.7 4.5 %fusion.27 = (bf16[12,9,128,64]{3,2,1,0:T(8,128)(2,1)S(1)}, bf16[12,9,128,64]{3,2,1,0:T(8,128)(2,1)S(1)}) fusion(bf16[12,9,128,128]{3,2,1,0:T(8,128)(2,1)} %bitcast.32), kind=kLoop, calls=%fused_computation.50 | loop fusion | bytes 7077888 | tf_op jit(solution)/shard_map/slice | solution.py:45
  72.2 1.3 %select_reduce_fusion = (f32[12,128]{1,0:T(8,128)S(1)}, f32[12,128,1152]{2,1,0:T(8,128)S(1)}) fusion(pred[12,1152]{1,0:T(8,128)(4,1)S(1)} %bitcast.39, bf16[12,128,64]{2,1,0:T(8,128)(2,1)S(1)} %bitcast.35, bf16[12,1152,64]{2,1,0:T(8,128)(2,1)S(1)} %bitcast.34), kind=kOutput, calls=%fused_computation.7 | convolution fusion | flops 230029824 | bytes 9063936 | tf_op jit(solution)/shard_map/ltv,lpv->ltp/dot_general | solution.py:47
  73.5 1.7 %fusion.3 = f32[12,128]{1,0:T(8,128)S(1)} fusion(f32[12,128,1152]{2,1,0:T(8,128)S(1)} %get-tuple-element.20, f32[12,128]{1,0:T(8,128)S(1)} %get-tuple-element.19, pred[12,1152]{1,0:T(8,128)(4,1)S(1)} %bitcast.40), kind=kLoop, calls=%fused_computation.11 | loop fusion | flops 5306880 | bytes 7104000 | tf_op jit(solution)/shard_map/reduce_sum | solution.py:54
  75.2 2.0 %fusion.17 = bf16[12,128,64]{1,2,0:T(8,128)(2,1)S(1)} fusion(bf16[12,1152,64]{2,1,0:T(8,128)(2,1)S(1)} %bitcast.36, f32[12,128,1152]{2,1,0:T(8,128)S(1)} %get-tuple-element.20, f32[12,128]{1,0:T(8,128)S(1)} %get-tuple-element.19, pred[12,1152]{1,0:T(8,128)(4,1)S(1)} %bitcast.41, f32[12,128]{1,0:T(8,128)S(1)} %fusion.3), kind=kOutput, calls=%fused_computation.22 | convolution fusion | flops 231997440 | bytes 9070080 | tf_op jit(solution)/shard_map/uct,uth->uch/dot_general | solution.py:56
  77.6 11.6 %all_to_all.19 = bf16[4,384,64]{1,2,0:T(8,128)(2,1)S(1)} all-to-all(bf16[4,384,64]{1,2,0:T(8,128)(2,1)S(1)} %pad_maximum_fusion.2), channel_id=1, replica_groups=mesh['space'=8,'mp'=4] {'mp'}, dimensions={0} | all-to-all | bytes 393216 | tf_op jit(solution)/shard_map/all_to_all | solution.py:100
  89.2 1.3 %convolution_convert_fusion = bf16[384,1024]{1,0:T(8,128)(2,1)} fusion(bf16[384,256]{0,1:T(8,128)(2,1)S(1)} %bitcast.38, bf16[256,1024]{1,0:T(8,128)(2,1)S(1)} %copy-done), kind=kOutput, calls=%fused_computation.20 | convolution fusion | flops 201719808 | bytes 1507328 | tf_op jit(solution)/shard_map/dot_general | solution.py:102
  (45 shorter events, 1.0 us)
Async XLA Ops:
  0.0 89.2 %copy-start = (bf16[256,1024]{1,0:T(8,128)(2,1)S(1)}, bf16[256,1024]{1,0:T(8,128)(2,1)}, u32[]{:S(2)}) copy-start(bf16[256,1024]{1,0:T(8,128)(2,1)} %param.10) | copy-start | bytes 1572868
  0.0 5.8 %copy-start.1 = (s32[1536]{0:T(1024)S(1)}, s32[1536]{0:T(1024)}, u32[]{:S(2)}) copy-start(s32[1536]{0:T(1024)} %param.12) | copy-start | bytes 18436
  5.8 16.9 %copy-start.4 = (bf16[1024,1,192]{0,2,1:T(8,128)(2,1)S(1)}, bf16[1024,1,192]{0,2,1:T(8,128)(2,1)}, u32[]{:S(2)}) copy-start(bf16[1024,1,192]{0,2,1:T(8,128)(2,1)} %param.9) | copy-start | bytes 1179652
  5.8 16.9 %copy-start.5 = (f32[1024]{0:T(1024)S(1)}, f32[1024]{0:T(1024)}, u32[]{:S(2)}) copy-start(f32[1024]{0:T(1024)} %param.8) | copy-start | bytes 12292
  14.9 17.5 %all-to-all-start = ((s32[8,1,192]{2,1,0:T(1,128)}), s32[8,1,192]{2,1,0:T(1,128)S(1)}, u32[]{:S(2)}, u32[]{:S(2)}) async-start(s32[8,1,192]{2,1,0:T(1,128)} %all_to_all.12), calls=%async_computation | async-start | bytes 16384 | tf_op jit(solution)/shard_map/all_to_all | solution.py:76
  27.1 9.6 %copy-start.3 = (s32[12,9]{1,0:T(8,128)S(1)}, s32[12,9]{1,0:T(8,128)}, u32[]{:S(2)}) copy-start(s32[12,9]{1,0:T(8,128)} %param.13) | copy-start | bytes 1300
  32.4 16.8 %all-to-all-start.1 = ((bf16[8,192,192]{2,1,0:T(8,128)(2,1)}), bf16[8,192,192]{2,1,0:T(8,128)(2,1)S(1)}, u32[]{:S(2)}, u32[]{:S(2)}) async-start(bf16[8,192,192]{2,1,0:T(8,128)(2,1)} %bitcast.2), calls=%async_computation.1 | async-start | bytes 1572864 | tf_op jit(solution)/shard_map/all_to_all | solution.py:75
  56.5 11.2 %copy-start.2 = (bf16[1536,192]{1,0:T(8,128)(2,1)}, bf16[1536,192]{1,0:T(8,128)(2,1)S(1)}, u32[]{:S(2)}) copy-start(bf16[1536,192]{1,0:T(8,128)(2,1)S(1)} %scatter_custom_fusion) | copy-start | bytes 1769476
  56.7 8.1 %collective-permute-start = (bf16[768,128]{1,0:T(8,128)(2,1)S(1)}, bf16[768,128]{1,0:T(8,128)(2,1)S(1)}, u32[]{:S(2)}, u32[]{:S(2)}) collective-permute-start(bf16[768,128]{1,0:T(8,128)(2,1)S(1)} %get-tuple-element.13), channel_id=1, source_target_pairs={{0,4},{4,8},{8,12},{12,16},{16,20},{20,24},{24,28},{28,0},{1,5},{5... | collective-permute-start | bytes 589832 | tf_op jit(solution)/shard_map/ppermute | solution.py:17
  56.8 8.1 %collective-permute-start.1 = (bf16[768,128]{1,0:T(8,128)(2,1)S(1)}, bf16[768,128]{1,0:T(8,128)(2,1)S(1)}, u32[]{:S(2)}, u32[]{:S(2)}) collective-permute-start(bf16[768,128]{1,0:T(8,128)(2,1)S(1)} %get-tuple-element.14), channel_id=1, source_target_pairs={{4,0},{8,4},{12,8},{16,12},{20,16},{24,20},{28,24},{0,28},{5,1},{9... | collective-permute-start | bytes 589832 | tf_op jit(solution)/shard_map/ppermute | solution.py:18
  67.7 4.5 %slice-start = ((bf16[1536,192]{1,0:T(8,128)(2,1)}), bf16[1536,64]{1,0:T(8,128)(2,1)S(1)}, s32[]{:S(2)}) async-start(bf16[1536,192]{1,0:T(8,128)(2,1)} %copy-done.2), calls=%async_computation.3 | async-start | bytes 786432 | tf_op jit(solution)/shard_map/slice | solution.py:82
